TPU v7x, 512 devices: a whole 4x8x8 slice. The times are simulated.
512 devices in a mesh: py: 32 (over y, x), pz: 16 (over z, core).
Axes of the slice: x: 4, y: 8, z: 8, core: 2. Of those that a mesh axis runs over, the one named last changes fastest.
Arguments:
- velocity: float32 [3, 32, 1024, 1024], P(None, 'py', 'pz'), may hold values from -14 to 14
Outputs:
- nu_t: float32 [32, 1024, 1024], P('py', 'pz')
- filtered_velocity: bfloat16 [3, 32, 1024, 1024], P(None, 'py', None, 'pz')
All inputs are finite; a program needn't handle non-finite values.
Results may differ from a plain program's by a relative error of at most 0.012.
The roundings to bfloat16 on the way count: a program that leaves them out, or rounds other values in their place, can miss the bound.
Values may be sent and summed in bfloat16 or wider, within the bound.
No kernel may reach another device: no remote copies, remote signals or barrier semaphores. Data moves between devices by JAX's collectives and lax.ppermute only.
A program may use at most 64 MiB of HBM per device.

v0:
```python
import math
import jax
import jax.numpy as jnp
import numpy as np
from jax import lax
from jax.sharding import PartitionSpec as P

index_pairs = ((0, 0), (1, 1), (2, 2), (0, 1), (0, 2), (1, 2))
pair_weights = (1.0, 1.0, 1.0, 2.0, 2.0, 2.0)
epsilon = 1e-06


def extended(x, sides, width):
    edges = {}
    for axis, dim in sides:
        devices, length = (lax.axis_size(axis), x.shape[dim])
        up = [(i, (i + 1) % devices) for i in range(devices)]
        last = lax.slice_in_dim(x, length - width, length, axis=dim)
        initial = lax.slice_in_dim(x, 0, width, axis=dim)
        edges[dim] = (
            lax.ppermute(last, axis, up),
            lax.ppermute(initial, axis, [(b, a) for a, b in up]),
        )
    done = []
    for _, dim in sides:
        low, high = edges[dim]
        around = [(width, width) if d in done else (0, 0) for d in range(x.ndim)]
        x = jnp.concatenate([jnp.pad(low, around), x, jnp.pad(high, around)], axis=dim)
        done.append(dim)
    return x


def copy_for_each(x, axis):
    copies = jnp.broadcast_to(x, (lax.axis_size(axis), *x.shape))
    return lax.all_to_all(copies, axis, split_axis=0, concat_axis=0, tiled=True)


def taken_together(x, axis):
    return copy_for_each(x, axis).sum(axis=0)


def packed_total(arrays, axis):
    line, at, gathered = (jnp.concatenate([a.reshape(-1) for a in arrays]), 0, [])
    running = taken_together(line, axis)
    for a in arrays:
        gathered.append(running[at : at + a.size].reshape(a.shape))
        at += a.size
    return tuple(gathered)


def filter_table(length):
    offsets = np.arange(length, dtype=np.int64)
    wavenumbers = np.arange(1, length // 4, dtype=np.int64)
    phase = offsets[:, None] * wavenumbers[None, :] % length
    kernel = (1.0 + 2.0 * np.cos(phase * (2.0 * math.pi / length)).sum(axis=1)) / length
    kernel = kernel.astype(np.float32)
    lagged = (offsets[:, None] - offsets[None, :]) % length
    return jnp.asarray(kernel[lagged], dtype=jnp.float32).astype(jnp.bfloat16)


def seal_walls(padded):
    device_index = lax.axis_index("py")
    last_index = lax.axis_size("py") - 1
    lower_rim = jnp.where(device_index == 0, jnp.zeros_like(padded[:, :1]), padded[:, :1])
    upper_rim = jnp.where(
        device_index == last_index, jnp.zeros_like(padded[:, -1:]), padded[:, -1:]
    )
    return jnp.concatenate([lower_rim, padded[:, 1:-1], upper_rim], axis=1)


def derivatives(padded, rim_axis):
    padded = padded.astype(jnp.float32)
    if rim_axis == 2:
        interior = padded[:, 1:-1, 1:-1, :]
        slope_rim = (padded[:, 1:-1, 2:, :] - padded[:, 1:-1, :-2, :]) * 0.5
        slope_roll = (jnp.roll(interior, -1, 3) - jnp.roll(interior, 1, 3)) * 0.5
        slope_y = (padded[:, 2:, 1:-1, :] - padded[:, :-2, 1:-1, :]) * 0.5
        return (slope_roll, slope_y, slope_rim)
    interior = padded[:, 1:-1, :, 1:-1]
    slope_rim = (padded[:, 1:-1, :, 2:] - padded[:, 1:-1, :, :-2]) * 0.5
    slope_roll = (jnp.roll(interior, -1, 2) - jnp.roll(interior, 1, 2)) * 0.5
    slope_y = (padded[:, 2:, :, 1:-1] - padded[:, :-2, :, 1:-1]) * 0.5
    return (slope_rim, slope_y, slope_roll)


def strain(gradients):
    strain_parts = [0.5 * (gradients[b][a] + gradients[a][b]) for a, b in index_pairs]
    squares_sum = pair_weights[0] * strain_parts[0] * strain_parts[0]
    for weight, part_value in zip(pair_weights[1:], strain_parts[1:]):
        squares_sum = squares_sum + weight * part_value * part_value
    return (strain_parts, jnp.sqrt(2.0 * squares_sum))


def lilly_sums(filtered, padded_hat, rim_axis):
    hat_parts, magnitude_hat = strain(derivatives(padded_hat, rim_axis))
    smooth_velocity = filtered[:3].astype(jnp.float32)
    numerator = jnp.zeros_like(magnitude_hat)
    denominator = jnp.zeros_like(magnitude_hat)
    for pair_index, (a, b) in enumerate(index_pairs):
        leonard = (
            filtered[3 + pair_index].astype(jnp.float32) - smooth_velocity[a] * smooth_velocity[b]
        )
        model_term = (
            filtered[9 + pair_index].astype(jnp.float32)
            - 4.0 * magnitude_hat * hat_parts[pair_index]
        )
        numerator = numerator + pair_weights[pair_index] * leonard * model_term
        denominator = denominator + pair_weights[pair_index] * model_term * model_term
    return (jnp.sum(numerator, axis=(1, 2)), jnp.sum(denominator, axis=(1, 2)))


def body(velocity):
    padded = extended(velocity, (("py", 1), ("pz", 2)), 1)
    strain_parts, magnitude = strain(derivatives(seal_walls(padded), 2))
    pieces = [velocity[a].astype(jnp.bfloat16) for a in range(3)]
    pieces = pieces + [(velocity[a] * velocity[b]).astype(jnp.bfloat16) for a, b in index_pairs]
    pieces = pieces + [(magnitude * part_value).astype(jnp.bfloat16) for part_value in strain_parts]
    fields = jnp.stack(pieces)
    table_x = filter_table(velocity.shape[3])
    table_z = filter_table(velocity.shape[2] * lax.axis_size("pz"))
    along_x = jnp.einsum(
        "fyzx,xv->fyzv", fields, table_x, preferred_element_type=jnp.float32
    ).astype(jnp.bfloat16)
    filtered = jnp.einsum(
        "wz,fyzx->fywx",
        table_z,
        lax.all_to_all(along_x, "pz", split_axis=3, concat_axis=2, tiled=True),
        preferred_element_type=jnp.float32,
    ).astype(jnp.bfloat16)
    padded_hat = extended(filtered[:3], (("py", 1), ("pz", 3)), 1)
    numerator, denominator = lilly_sums(filtered, seal_walls(padded_hat), 3)
    numerator, denominator = packed_total((numerator, denominator), "pz")
    plane_cells = velocity.shape[3] * velocity.shape[2] * lax.axis_size("pz")
    coefficient = numerator / plane_cells / (2.0 * (denominator / plane_cells + epsilon))
    nu_t = coefficient[:, None, None] * magnitude
    return (nu_t, filtered[:3])


def solution(mesh):
    in_specs = (P(None, "py", "pz", None),)
    out_specs = (P("py", "pz", None), P(None, "py", None, "pz"))
    return jax.shard_map(body, mesh=mesh, in_specs=in_specs, out_specs=out_specs, check_vma=False)
```

profile of v0, /device:TPU:1, one launch (start us, length us, event | category | flops | bytes accessed | tf_op | source)
XLA Modules:
  0.0 176.1 jit_solution(13759545348752628538)
XLA Ops:
  0.6 4.1 %collective-permute-start.1 = (f32[3,1,64,1024]{3,2,1,0:T(8,128)}, f32[3,1,64,1024]{3,2,1,0:T(8,128)S(1)}, u32[]{:S(2)}, u32[]{:S(2)}) collective-permute-start(f32[3,1,64,1024]{3,2,1,0:T(8,128)} %param.3), channel_id=1, source_target_pairs={{0,16},{16,32},{32,48},{48,64},{64,80},{80,96},{96,112},{112,128},... | collective-permute-start | bytes 2359304 | tf_op jit(solution)/shard_map/ppermute | solution.py:21
  4.7 6.1 %collective-permute-start.2 = (f32[3,1,64,1024]{3,2,1,0:T(8,128)}, f32[3,1,64,1024]{3,2,1,0:T(8,128)S(1)}, u32[]{:S(2)}, u32[]{:S(2)}) collective-permute-start(f32[3,1,64,1024]{3,2,1,0:T(8,128)} %param.3), channel_id=1, source_target_pairs={{16,0},{32,16},{48,32},{64,48},{80,64},{96,80},{112,96},{128,112},... | collective-permute-start | bytes 2359304 | tf_op jit(solution)/shard_map/ppermute | solution.py:22
  10.8 1.0 fusion.91
  11.8 2.9 %collective-permute-start = (f32[3,1,1,1024]{3,2,1,0:T(1,128)S(1)}, f32[3,1,1,1024]{3,2,1,0:T(1,128)S(1)}, u32[]{:S(2)}, u32[]{:S(2)}) collective-permute-start(f32[3,1,1,1024]{3,2,1,0:T(1,128)S(1)} %get-tuple-element.24), channel_id=1, source_target_pairs={{0,1},{1,2},{2,3},{3,4},{4,5},{5,6},{6,7},{7,8},{8,9},{9,10},{10,1... | collective-permute-start | bytes 36872 | tf_op jit(solution)/shard_map/ppermute | solution.py:21
  14.7 3.1 %collective-permute-start.3 = (f32[3,1,1,1024]{3,2,1,0:T(1,128)S(1)}, f32[3,1,1,1024]{3,2,1,0:T(1,128)S(1)}, u32[]{:S(2)}, u32[]{:S(2)}) collective-permute-start(f32[3,1,1,1024]{3,2,1,0:T(1,128)S(1)} %get-tuple-element.25), channel_id=1, source_target_pairs={{1,0},{2,1},{3,2},{4,3},{5,4},{6,5},{7,6},{8,7},{9,8},{10,9},{11,1... | collective-permute-start | bytes 36872 | tf_op jit(solution)/shard_map/ppermute | solution.py:22
  17.8 1.0 fusion.66
  18.8 1.0 fusion.67
  19.8 1.0 fusion.68
  20.8 1.0 fusion.69
  21.7 1.0 fusion.70
  22.7 1.0 fusion.71
  23.8 1.3 copy-done.2
  25.1 0.1 fusion.92
  25.2 0.3 fusion.93
  25.5 0.3 fusion.16
  26.0 0.1 constant_dynamic-update-slice_fusion.1
  26.1 0.3 fusion.11
  26.4 1.2 copy-done.3
  27.7 0.3 fusion.79
  28.2 1.3 copy-done.4
  29.5 3.5 %convert_bitcast_fusion = bf16[15,1,64,1024]{3,2,0,1:T(8,128)(2,1)} fusion(bf16[1024,1024,1]{1,0,2:T(8,128)(2,1)S(1)} %copy-done.4, bf16[15,1,64,1024]{3,2,0,1:T(8,128)(2,1)S(1)} %fusion.80), kind=kOutput, calls=%fused_computation.6 | convolution fusion | flops 2014248960 | bytes 6029312 | tf_op jit(solution)/shard_map/fyzx,xv->fyzv/dot_general | solution.py:121
  33.0 6.2 %copy.154 = bf16[15,1,64,1024]{2,0,1,3:T(8,128)(2,1)} copy(bf16[15,1,64,1024]{3,2,0,1:T(8,128)(2,1)} %convert_bitcast_fusion) | data formatting | bytes 3932160 | tf_op jit(solution)/shard_map/convert_element_type | solution.py:123
  39.2 7.3 %reshape.1162 = bf16[16,2,30720]{2,1,0:T(2,128)(2,1)} reshape(bf16[1024,1,15,64]{3,2,1,0:T(8,128)(2,1)} %bitcast.264) | data formatting | bytes 3932160
  46.5 61.5 %all_to_all.21 = bf16[16,2,30720]{2,1,0:T(2,128)(2,1)} all-to-all(bf16[16,2,30720]{2,1,0:T(2,128)(2,1)} %reshape.1162), channel_id=1, replica_groups=mesh['py'=32,'pz'=16] {'pz'}, dimensions={0} | all-to-all | bytes 3932160 | tf_op jit(solution)/shard_map/all_to_all | solution.py:127
  108.0 7.5 %reshape.1163 = bf16[1024,1,15,64]{3,2,1,0:T(8,128)(2,1)} reshape(bf16[16,2,30720]{2,1,0:T(2,128)(2,1)} %all_to_all.21) | data formatting | bytes 3932160
  115.5 5.8 %copy.155 = bf16[15,1,64,1024]{3,2,0,1:T(8,128)(2,1)} copy(bf16[15,1,64,1024]{2,0,1,3:T(8,128)(2,1)} %bitcast.265) | data formatting | bytes 3932160 | tf_op jit(solution)/shard_map/all_to_all | solution.py:127
  121.2 6.1 %reshape.1156 = bf16[15,1024,64]{2,1,0:T(8,128)(2,1)} reshape(bf16[15,1,64,1024]{3,2,0,1:T(8,128)(2,1)} %copy.155) | data formatting | bytes 3932160 | tf_op jit(solution)/shard_map/wz,fyzx->fywx/dot_general | solution.py:124
  127.3 7.0 %convolution_convert_fusion = bf16[15,64,1024]{2,1,0:T(8,128)(2,1)S(1)} fusion(bf16[15,1024,64]{2,1,0:T(8,128)(2,1)} %reshape.1156, bf16[1024,1024,1]{1,0,2:T(8,128)(2,1)} %constant.58), kind=kOutput, calls=%fused_computation.7 | convolution fusion | flops 2014248960 | bytes 6029312 | tf_op jit(solution)/shard_map/wz,fyzx->fywx/dot_general | solution.py:124
  134.3 0.1 fusion.87
  134.4 7.3 %collective-permute-start.6 = (bf16[3,1,1024,64]{2,3,1,0:T(8,128)(2,1)S(1)}, bf16[3,1,1024,64]{2,3,1,0:T(8,128)(2,1)S(1)}, u32[]{:S(2)}, u32[]{:S(2)}) collective-permute-start(bf16[3,1,1024,64]{2,3,1,0:T(8,128)(2,1)S(1)} %get-tuple-element.8), channel_id=1, source_target_pairs={{16,0},{32,16},{48,32},{64,48},{80,64},{96,80},{112,96},{128,112},... | collective-permute-start | bytes 1179656 | tf_op jit(solution)/shard_map/ppermute | solution.py:22
  141.8 1.9 %collective-permute-start.5 = (bf16[3,1,1024,64]{2,3,1,0:T(8,128)(2,1)S(1)}, bf16[3,1,1024,64]{2,3,1,0:T(8,128)(2,1)S(1)}, u32[]{:S(2)}, u32[]{:S(2)}) collective-permute-start(bf16[3,1,1024,64]{2,3,1,0:T(8,128)(2,1)S(1)} %get-tuple-element.8), channel_id=1, source_target_pairs={{0,16},{16,32},{32,48},{48,64},{64,80},{80,96},{96,112},{112,128},... | collective-permute-start | bytes 1179656 | tf_op jit(solution)/shard_map/ppermute | solution.py:21
  143.8 0.5 collective-permute-start.7
  144.3 0.7 collective-permute-done.4
  144.9 2.3 %collective-permute-done.7 = bf16[3,1,1024,1]{2,3,1,0:T(2,128)(2,1)S(1)} collective-permute-done((bf16[3,1,1024,1]{2,3,1,0:T(2,128)(2,1)S(1)}, bf16[3,1,1024,1]{2,3,1,0:T(2,128)(2,1)S(1)}, u32[]{:S(2)}, u32[]{:S(2)}) %collective-permute-start.7) | collective-permute-done | bytes 6176 | tf_op jit(solution)/shard_map/ppermute | solution.py:22
  147.2 3.2 %collective-permute-done.6 = bf16[3,1,1024,64]{2,3,1,0:T(8,128)(2,1)S(1)} collective-permute-done((bf16[3,1,1024,64]{2,3,1,0:T(8,128)(2,1)S(1)}, bf16[3,1,1024,64]{2,3,1,0:T(8,128)(2,1)S(1)}, u32[]{:S(2)}, u32[]{:S(2)}) %collective-permute-start.6) | collective-permute-done | bytes 393248 | tf_op jit(solution)/shard_map/ppermute | solution.py:22
  150.4 7.7 %collective-permute-done.5 = bf16[3,1,1024,64]{2,3,1,0:T(8,128)(2,1)S(1)} collective-permute-done((bf16[3,1,1024,64]{2,3,1,0:T(8,128)(2,1)S(1)}, bf16[3,1,1024,64]{2,3,1,0:T(8,128)(2,1)S(1)}, u32[]{:S(2)}, u32[]{:S(2)}) %collective-permute-start.5) | collective-permute-done | bytes 393248 | tf_op jit(solution)/shard_map/ppermute | solution.py:21
  158.1 0.4 fusion.6
  158.5 0.1 slice_select_fusion.1
  158.6 0.1 maximum_convert_fusion.1
  158.7 0.2 maximum_convert_fusion
  159.0 0.3 fusion.89
  159.3 0.6 fusion.8
  159.9 1.4 fusion.59
  161.3 0.8 fusion.38
  162.1 1.3 pad_maximum_fusion.6
  163.4 9.8 %all_to_all.22 = f32[16,1,2]{2,1,0:T(1,128)S(1)} all-to-all(f32[16,1,2]{2,1,0:T(1,128)S(1)} %broadcast_in_dim.4), channel_id=1, replica_groups=mesh['py'=32,'pz'=16] {'pz'}, dimensions={0} | all-to-all | bytes 256 | tf_op jit(solution)/shard_map/all_to_all | solution.py:35
  173.3 0.6 fusion.94
  175.1 1.0 fusion.44
  (27 shorter events, 0.6 us)
Async XLA Ops:
  0.6 23.0 %copy-start = (f32[3,1,64,1024]{3,2,1,0:T(8,128)S(1)}, f32[3,1,64,1024]{3,2,1,0:T(8,128)}, u32[]{:S(2)}) copy-start(f32[3,1,64,1024]{3,2,1,0:T(8,128)} %param.3) | copy-start | bytes 2359300
  0.6 25.3 %collective-permute-start.1 = (f32[3,1,64,1024]{3,2,1,0:T(8,128)}, f32[3,1,64,1024]{3,2,1,0:T(8,128)S(1)}, u32[]{:S(2)}, u32[]{:S(2)}) collective-permute-start(f32[3,1,64,1024]{3,2,1,0:T(8,128)} %param.3), channel_id=1, source_target_pairs={{0,16},{16,32},{32,48},{48,64},{64,80},{80,96},{96,112},{112,128},... | collective-permute-start | bytes 2359304 | tf_op jit(solution)/shard_map/ppermute | solution.py:21
  4.7 21.3 %collective-permute-start.2 = (f32[3,1,64,1024]{3,2,1,0:T(8,128)}, f32[3,1,64,1024]{3,2,1,0:T(8,128)S(1)}, u32[]{:S(2)}, u32[]{:S(2)}) collective-permute-start(f32[3,1,64,1024]{3,2,1,0:T(8,128)} %param.3), channel_id=1, source_target_pairs={{16,0},{32,16},{48,32},{64,48},{80,64},{96,80},{112,96},{128,112},... | collective-permute-start | bytes 2359304 | tf_op jit(solution)/shard_map/ppermute | solution.py:22
  11.8 14.1 %collective-permute-start = (f32[3,1,1,1024]{3,2,1,0:T(1,128)S(1)}, f32[3,1,1,1024]{3,2,1,0:T(1,128)S(1)}, u32[]{:S(2)}, u32[]{:S(2)}) collective-permute-start(f32[3,1,1,1024]{3,2,1,0:T(1,128)S(1)} %get-tuple-element.24), channel_id=1, source_target_pairs={{0,1},{1,2},{2,3},{3,4},{4,5},{5,6},{6,7},{7,8},{8,9},{9,10},{10,1... | collective-permute-start | bytes 36872 | tf_op jit(solution)/shard_map/ppermute | solution.py:21
  14.7 11.1 %collective-permute-start.3 = (f32[3,1,1,1024]{3,2,1,0:T(1,128)S(1)}, f32[3,1,1,1024]{3,2,1,0:T(1,128)S(1)}, u32[]{:S(2)}, u32[]{:S(2)}) collective-permute-start(f32[3,1,1,1024]{3,2,1,0:T(1,128)S(1)} %get-tuple-element.25), channel_id=1, source_target_pairs={{1,0},{2,1},{3,2},{4,3},{5,4},{6,5},{7,6},{8,7},{9,8},{10,9},{11,1... | collective-permute-start | bytes 36872 | tf_op jit(solution)/shard_map/ppermute | solution.py:22
  23.8 1.3 copy-start.2
  26.1 1.5 copy-start.3
  27.9 1.6 copy-start.4
  134.4 24.2 %copy-start.1 = (bf16[3,1,1024,64]{2,3,1,0:T(8,128)(2,1)}, bf16[3,1,1024,64]{2,3,1,0:T(8,128)(2,1)S(1)}, u32[]{:S(2)}) copy-start(bf16[3,1,1024,64]{2,3,1,0:T(8,128)(2,1)S(1)} %get-tuple-element.8) | copy-start | bytes 1179652
  134.4 16.0 %collective-permute-start.6 = (bf16[3,1,1024,64]{2,3,1,0:T(8,128)(2,1)S(1)}, bf16[3,1,1024,64]{2,3,1,0:T(8,128)(2,1)S(1)}, u32[]{:S(2)}, u32[]{:S(2)}) collective-permute-start(bf16[3,1,1024,64]{2,3,1,0:T(8,128)(2,1)S(1)} %get-tuple-element.8), channel_id=1, source_target_pairs={{16,0},{32,16},{48,32},{64,48},{80,64},{96,80},{112,96},{128,112},... | collective-permute-start | bytes 1179656 | tf_op jit(solution)/shard_map/ppermute | solution.py:22
  141.8 16.3 %collective-permute-start.5 = (bf16[3,1,1024,64]{2,3,1,0:T(8,128)(2,1)S(1)}, bf16[3,1,1024,64]{2,3,1,0:T(8,128)(2,1)S(1)}, u32[]{:S(2)}, u32[]{:S(2)}) collective-permute-start(bf16[3,1,1024,64]{2,3,1,0:T(8,128)(2,1)S(1)} %get-tuple-element.8), channel_id=1, source_target_pairs={{0,16},{16,32},{32,48},{48,64},{64,80},{80,96},{96,112},{112,128},... | collective-permute-start | bytes 1179656 | tf_op jit(solution)/shard_map/ppermute | solution.py:21
  143.7 1.2 collective-permute-start.4
  143.8 3.4 %collective-permute-start.7 = (bf16[3,1,1024,1]{2,3,1,0:T(2,128)(2,1)S(1)}, bf16[3,1,1024,1]{2,3,1,0:T(2,128)(2,1)S(1)}, u32[]{:S(2)}, u32[]{:S(2)}) collective-permute-start(bf16[3,1,1024,1]{2,3,1,0:T(2,128)(2,1)S(1)} %get-tuple-element.18), channel_id=1, source_target_pairs={{1,0},{2,1},{3,2},{4,3},{5,4},{6,5},{7,6},{8,7},{9,8},{10,9},{11,1... | collective-permute-start | bytes 18440 | tf_op jit(solution)/shard_map/ppermute | solution.py:22
where the time goes:
time: 177 us; the launch traced here: 176 us
  blocking collectives  71.3 us (40%)
  local copies, waits for them, and re-layouts  42 us (24%)
  starting transfers between devices  26 us (15%)
  waiting for transfers between devices  13.9 us (8%)
  matrix products  10.5 us (6%)
  other arithmetic  10.2 us (6%)
  between operations  2.21 us (1%)
    all_to_all x1, blocking collectives, body(): lax.all_to_all(along_x, 'pz', split_axis=3, concat_axis=2, tiled=True)  61.5 us
    unnamed x17, local copies, waits for them, and re-layouts  21.6 us
    ppermute x4, starting transfers between devices, extended(): lax.ppermute(initial, axis, [(b, a) for a, b in up])  17 us
    all_to_all x1, blocking collectives, copy_for_each(): return lax.all_to_all(copies, axis, split_axis=0, concat_axis=0, tiled=True)  9.84 us
    ppermute x4, starting transfers between devices, extended(): lax.ppermute(last, axis, up)  8.97 us
    ppermute x4, waiting for transfers between devices, extended(): lax.ppermute(last, axis, up)  8.38 us
    dot_general x1, matrix products, body(): jnp.einsum('wz,fyzx->fywx', table_z, lax.all_to_all(along_x, 'pz', split_...  7.04 us
    convert_element_type x1, local copies, waits for them, and re-layouts, body(): along_x = jnp.einsum('fyzx,xv->fyzv', fields, table_x, preferred_element_...  6.18 us
  transfers between devices with their start and end apart: 8, of which 4 were waited for; matrix products, arithmetic and copies ran while one was open for 4% of the time, Pallas kernels for 0%

commit v1 on v0

--- a/solution.py
+++ b/solution.py
@@ -8,6 +8,15 @@
 index_pairs = ((0, 0), (1, 1), (2, 2), (0, 1), (0, 2), (1, 2))
 pair_weights = (1.0, 1.0, 1.0, 2.0, 2.0, 2.0)
 epsilon = 1e-06
+
+
+def _show_loads(vec, mesh_dim="pz"):
+    local_part = lax.axis_size(mesh_dim)
+    vec_out = jnp.split(vec, local_part, axis=3)
+    after = jnp.stack(vec_out)
+    kept_arr = lax.all_to_all(after, split_axis=0, concat_axis=0, axis_name=mesh_dim)
+    z_new = jnp.concatenate(kept_arr, axis=2)
+    return z_new
 
 
 def extended(x, sides, width):
@@ -122,10 +131,7 @@
         "fyzx,xv->fyzv", fields, table_x, preferred_element_type=jnp.float32
     ).astype(jnp.bfloat16)
     filtered = jnp.einsum(
-        "wz,fyzx->fywx",
-        table_z,
-        lax.all_to_all(along_x, "pz", split_axis=3, concat_axis=2, tiled=True),
-        preferred_element_type=jnp.float32,
+        "wz,fyzx->fywx", table_z, _show_loads(along_x), preferred_element_type=jnp.float32
     ).astype(jnp.bfloat16)
     padded_hat = extended(filtered[:3], (("py", 1), ("pz", 3)), 1)
     numerator, denominator = lilly_sums(filtered, seal_walls(padded_hat), 3)

time: 177 us -> 177 us (level)
  local copies, waits for them, and re-layouts: 42 us -> 46.5 us
  matrix products: 10.5 us -> 6.6 us
    reshape x0 -> x2, local copies, waits for them, and re-layouts: none -> 11.6 us  [_show_loads(): z_new = jnp.concatenate(kept_arr, axis=2)]
    another operation x0 -> x2, local copies, waits for them, and re-layouts: none -> 6.39 us
    convert_element_type x1 -> x0, local copies, waits for them, and re-layouts: 6.18 us -> none  [body(): along_x = jnp.einsum('fyzx,xv->fyzv', fields, table_x, preferred_element_...]
    dot_general x1 -> x0, local copies, waits for them, and re-layouts: 6.05 us -> none  [body(): jnp.einsum('wz,fyzx->fywx', table_z, lax.all_to_all(along_x, 'pz', split_...]
    all_to_all x1 -> x0, local copies, waits for them, and re-layouts: 5.76 us -> none  [body(): lax.all_to_all(along_x, 'pz', split_axis=3, concat_axis=2, tiled=True)]
    unnamed x17 -> x34, local copies, waits for them, and re-layouts: 21.6 us -> 26.2 us
    dot_general x1, matrix products: 7.04 us -> 4.41 us  [body(): jnp.einsum('wz,fyzx->fywx', table_z, _show_loads(along_x), preferred_elem...]
  transfers between devices with their start and end apart: 8 -> 8, of which waited for: 4 -> 4; matrix products, arithmetic and copies ran while one was open for 4% -> 5% of each run, Pallas kernels for 0% -> 0%
where the time goes in v1:
time: 177 us; the launch traced here: 176 us
  blocking collectives  70.3 us (40%)
  local copies, waits for them, and re-layouts  46.5 us (26%)
  starting transfers between devices  25.9 us (15%)
  waiting for transfers between devices  13.9 us (8%)
  other arithmetic  10.4 us (6%)
  matrix products  6.6 us (4%)
  between operations  2.49 us (1%)
    all_to_all x1, blocking collectives, _show_loads(): lax.all_to_all(after, split_axis=0, concat_axis=0, axis_name=mesh_dim)  60.4 us
    unnamed x34, local copies, waits for them, and re-layouts  26.2 us
    ppermute x4, starting transfers between devices, extended(): lax.ppermute(initial, axis, [(b, a) for a, b in up])  16.9 us
    reshape x2, local copies, waits for them, and re-layouts, _show_loads(): z_new = jnp.concatenate(kept_arr, axis=2)  11.6 us
    all_to_all x1, blocking collectives, copy_for_each(): return lax.all_to_all(copies, axis, split_axis=0, concat_axis=0, tiled=True)  9.84 us
    ppermute x4, starting transfers between devices, extended(): lax.ppermute(last, axis, up)  8.97 us
    ppermute x4, waiting for transfers between devices, extended(): lax.ppermute(last, axis, up)  8.37 us
    another operation x1, local copies, waits for them, and re-layouts  6.22 us
  transfers between devices with their start and end apart: 8, of which 4 were waited for; matrix products, arithmetic and copies ran while one was open for 5% of the time, Pallas kernels for 0%

profile of v1, /device:TPU:1, one launch (start us, length us, event | category | flops | bytes accessed | tf_op | source)
XLA Modules:
  0.0 176.1 jit_solution(1779147420500811692)
XLA Ops:
  0.6 4.1 %collective-permute-start.1 = (f32[3,1,64,1024]{3,2,1,0:T(8,128)}, f32[3,1,64,1024]{3,2,1,0:T(8,128)}, u32[]{:S(2)}, u32[]{:S(2)}) collective-permute-start(f32[3,1,64,1024]{3,2,1,0:T(8,128)} %param.3), channel_id=1, source_target_pairs={{0,16},{16,32},{32,48},{48,64},{64,80},{80,96},{96,112},{112,128},... | collective-permute-start | bytes 2359304 | tf_op jit(solution)/shard_map/ppermute | solution.py:30
  4.7 6.1 %collective-permute-start.2 = (f32[3,1,64,1024]{3,2,1,0:T(8,128)}, f32[3,1,64,1024]{3,2,1,0:T(8,128)S(1)}, u32[]{:S(2)}, u32[]{:S(2)}) collective-permute-start(f32[3,1,64,1024]{3,2,1,0:T(8,128)} %param.3), channel_id=1, source_target_pairs={{16,0},{32,16},{48,32},{64,48},{80,64},{96,80},{112,96},{128,112},... | collective-permute-start | bytes 2359304 | tf_op jit(solution)/shard_map/ppermute | solution.py:31
  10.8 1.0 fusion.107
  11.8 2.9 %collective-permute-start = (f32[3,1,1,1024]{3,2,1,0:T(1,128)S(1)}, f32[3,1,1,1024]{3,2,1,0:T(1,128)S(1)}, u32[]{:S(2)}, u32[]{:S(2)}) collective-permute-start(f32[3,1,1,1024]{3,2,1,0:T(1,128)S(1)} %get-tuple-element.24), channel_id=1, source_target_pairs={{0,1},{1,2},{2,3},{3,4},{4,5},{5,6},{6,7},{7,8},{8,9},{9,10},{10,1... | collective-permute-start | bytes 36872 | tf_op jit(solution)/shard_map/ppermute | solution.py:30
  14.7 3.1 %collective-permute-start.3 = (f32[3,1,1,1024]{3,2,1,0:T(1,128)S(1)}, f32[3,1,1,1024]{3,2,1,0:T(1,128)S(1)}, u32[]{:S(2)}, u32[]{:S(2)}) collective-permute-start(f32[3,1,1,1024]{3,2,1,0:T(1,128)S(1)} %get-tuple-element.25), channel_id=1, source_target_pairs={{1,0},{2,1},{3,2},{4,3},{5,4},{6,5},{7,6},{8,7},{9,8},{10,9},{11,1... | collective-permute-start | bytes 36872 | tf_op jit(solution)/shard_map/ppermute | solution.py:31
  17.8 1.0 fusion.82
  18.8 1.0 fusion.83
  19.8 1.0 fusion.84
  20.8 1.0 fusion.85
  21.7 1.0 fusion.86
  22.7 1.0 fusion.87
  23.8 1.3 copy-done.3
  25.2 0.3 fusion.109
  25.5 0.3 fusion.16
  25.9 1.2 constant_dynamic-update-slice_fusion.2
  27.2 0.3 fusion.11
  27.6 1.2 copy-done.4
  28.8 0.3 fusion.95
  29.3 1.3 copy-done.5
  30.7 2.2 %convert_bitcast_fusion = bf16[15,1,64,1024]{3,2,0,1:T(8,128)(2,1)S(1)} fusion(bf16[1024,1024,1]{1,0,2:T(8,128)(2,1)S(1)} %copy-done.5, bf16[15,1,64,1024]{3,2,0,1:T(8,128)(2,1)S(1)} %fusion.96), kind=kOutput, calls=%fused_computation.6 | convolution fusion | flops 2014248960 | bytes 6029312 | tf_op jit(solution)/shard_map/fyzx,xv->fyzv/dot_general | solution.py:130
  32.9 0.2 fusion.80
  33.2 0.2 fusion.78
  33.5 0.2 fusion.76
  35.1 1.8 %copy-done.1 = bf16[16,15,1,64,64]{4,3,1,2,0:T(8,128)(2,1)} copy-done((bf16[16,15,1,64,64]{4,3,1,2,0:T(8,128)(2,1)}, bf16[16,15,1,64,64]{4,3,1,2,0:T(8,128)(2,1)S(1)}, u32[]{:S(2)}) %copy-start.1) | copy-done | bytes 1966104
  36.9 7.2 %reshape.1162 = bf16[16,2,30720]{2,1,0:T(2,128)(2,1)} reshape(bf16[16,1,15,64,64]{4,3,2,1,0:T(8,128)(2,1)} %bitcast.330) | data formatting | bytes 3932160
  44.1 60.4 %all_to_all.11 = bf16[16,2,30720]{2,1,0:T(2,128)(2,1)} all-to-all(bf16[16,2,30720]{2,1,0:T(2,128)(2,1)} %reshape.1162), channel_id=1, replica_groups=mesh['py'=32,'pz'=16] {'pz'}, dimensions={0} | all-to-all | bytes 3932160 | tf_op jit(solution)/shard_map/all_to_all | solution.py:17
  104.5 7.3 %reshape.1163 = bf16[16,1,15,64,64]{4,3,2,1,0:T(8,128)(2,1)} reshape(bf16[16,2,30720]{2,1,0:T(2,128)(2,1)} %all_to_all.11) | data formatting | bytes 3932160
  111.8 5.0 %bitcast_bitcast_fusion = bf16[15,1,16,64,64]{4,3,0,1,2:T(8,128)(2,1)} fusion(bf16[16,1,15,64,64]{4,3,2,1,0:T(8,128)(2,1)} %reshape.1163), kind=kLoop, calls=%fused_computation.201 | loop fusion | bytes 3932160 | tf_op jit(solution)/shard_map/reshape | solution.py:18
  116.8 6.6 %copy.117 = bf16[15,1,16,64,64]{3,2,4,0,1:T(8,128)(2,1)} copy(bf16[15,1,16,64,64]{4,3,0,1,2:T(8,128)(2,1)} %bitcast_bitcast_fusion) | data formatting | bytes 3932160 | tf_op jit(solution)/shard_map/reshape | solution.py:18
  123.4 6.2 %reshape.1153 = bf16[15,1024,64]{1,2,0:T(8,128)(2,1)} reshape(bf16[15,1,16,64,64]{3,2,4,0,1:T(8,128)(2,1)} %copy.117) | data formatting | bytes 3932160 | tf_op jit(solution)/shard_map/reshape.4
  129.6 4.4 %convolution_convert_fusion = bf16[15,64,1024]{2,1,0:T(8,128)(2,1)S(1)} fusion(bf16[15,1024,64]{1,2,0:T(8,128)(2,1)} %reshape.1153, bf16[1024,1024,1]{1,0,2:T(8,128)(2,1)} %constant.54), kind=kOutput, calls=%fused_computation.7 | convolution fusion | flops 2014248960 | bytes 6029312 | tf_op jit(solution)/shard_map/wz,fyzx->fywx/dot_general | solution.py:133
  134.1 7.2 %collective-permute-start.6 = (bf16[3,1,1024,64]{2,3,1,0:T(8,128)(2,1)S(1)}, bf16[3,1,1024,64]{2,3,1,0:T(8,128)(2,1)S(1)}, u32[]{:S(2)}, u32[]{:S(2)}) collective-permute-start(bf16[3,1,1024,64]{2,3,1,0:T(8,128)(2,1)S(1)} %get-tuple-element.8), channel_id=1, source_target_pairs={{16,0},{32,16},{48,32},{64,48},{80,64},{96,80},{112,96},{128,112},... | collective-permute-start | bytes 1179656 | tf_op jit(solution)/shard_map/ppermute | solution.py:31
  141.4 1.9 %collective-permute-start.5 = (bf16[3,1,1024,64]{2,3,1,0:T(8,128)(2,1)S(1)}, bf16[3,1,1024,64]{2,3,1,0:T(8,128)(2,1)S(1)}, u32[]{:S(2)}, u32[]{:S(2)}) collective-permute-start(bf16[3,1,1024,64]{2,3,1,0:T(8,128)(2,1)S(1)} %get-tuple-element.8), channel_id=1, source_target_pairs={{0,16},{16,32},{32,48},{48,64},{64,80},{80,96},{96,112},{112,128},... | collective-permute-start | bytes 1179656 | tf_op jit(solution)/shard_map/ppermute | solution.py:30
  143.4 0.5 collective-permute-start.7
  143.9 0.7 collective-permute-done.4
  144.5 2.3 %collective-permute-done.7 = bf16[3,1,1024,1]{2,3,1,0:T(2,128)(2,1)S(1)} collective-permute-done((bf16[3,1,1024,1]{2,3,1,0:T(2,128)(2,1)S(1)}, bf16[3,1,1024,1]{2,3,1,0:T(2,128)(2,1)S(1)}, u32[]{:S(2)}, u32[]{:S(2)}) %collective-permute-start.7) | collective-permute-done | bytes 6176 | tf_op jit(solution)/shard_map/ppermute | solution.py:31
  146.8 3.2 %collective-permute-done.6 = bf16[3,1,1024,64]{2,3,1,0:T(8,128)(2,1)S(1)} collective-permute-done((bf16[3,1,1024,64]{2,3,1,0:T(8,128)(2,1)S(1)}, bf16[3,1,1024,64]{2,3,1,0:T(8,128)(2,1)S(1)}, u32[]{:S(2)}, u32[]{:S(2)}) %collective-permute-start.6) | collective-permute-done | bytes 393248 | tf_op jit(solution)/shard_map/ppermute | solution.py:31
  150.0 7.7 %collective-permute-done.5 = bf16[3,1,1024,64]{2,3,1,0:T(8,128)(2,1)S(1)} collective-permute-done((bf16[3,1,1024,64]{2,3,1,0:T(8,128)(2,1)S(1)}, bf16[3,1,1024,64]{2,3,1,0:T(8,128)(2,1)S(1)}, u32[]{:S(2)}, u32[]{:S(2)}) %collective-permute-start.5) | collective-permute-done | bytes 393248 | tf_op jit(solution)/shard_map/ppermute | solution.py:30
  157.7 0.4 fusion.6
  158.3 0.2 maximum_convert_fusion
  158.5 0.3 fusion.105
  158.9 0.6 fusion.8
  159.5 1.4 fusion.59
  160.9 0.9 fusion.38
  161.8 1.4 pad_maximum_fusion.6
  163.2 9.8 %all_to_all.12 = f32[16,1,2]{2,1,0:T(1,128)S(1)} all-to-all(f32[16,1,2]{2,1,0:T(1,128)S(1)} %broadcast_in_dim.4), channel_id=1, replica_groups=mesh['py'=32,'pz'=16] {'pz'}, dimensions={0} | all-to-all | bytes 256 | tf_op jit(solution)/shard_map/all_to_all | solution.py:44
  173.1 0.6 fusion.110
  175.1 1.0 fusion.44
  (45 shorter events, 2.5 us)
Async XLA Ops:
  0.6 23.0 %copy-start = (f32[3,1,64,1024]{3,2,1,0:T(8,128)S(1)}, f32[3,1,64,1024]{3,2,1,0:T(8,128)}, u32[]{:S(2)}) copy-start(f32[3,1,64,1024]{3,2,1,0:T(8,128)} %param.3) | copy-start | bytes 2359300
  0.6 25.2 %collective-permute-start.1 = (f32[3,1,64,1024]{3,2,1,0:T(8,128)}, f32[3,1,64,1024]{3,2,1,0:T(8,128)}, u32[]{:S(2)}, u32[]{:S(2)}) collective-permute-start(f32[3,1,64,1024]{3,2,1,0:T(8,128)} %param.3), channel_id=1, source_target_pairs={{0,16},{16,32},{32,48},{48,64},{64,80},{80,96},{96,112},{112,128},... | collective-permute-start | bytes 2359304 | tf_op jit(solution)/shard_map/ppermute | solution.py:30
  4.7 22.4 %collective-permute-start.2 = (f32[3,1,64,1024]{3,2,1,0:T(8,128)}, f32[3,1,64,1024]{3,2,1,0:T(8,128)S(1)}, u32[]{:S(2)}, u32[]{:S(2)}) collective-permute-start(f32[3,1,64,1024]{3,2,1,0:T(8,128)} %param.3), channel_id=1, source_target_pairs={{16,0},{32,16},{48,32},{64,48},{80,64},{96,80},{112,96},{128,112},... | collective-permute-start | bytes 2359304 | tf_op jit(solution)/shard_map/ppermute | solution.py:31
  11.8 14.0 %collective-permute-start = (f32[3,1,1,1024]{3,2,1,0:T(1,128)S(1)}, f32[3,1,1,1024]{3,2,1,0:T(1,128)S(1)}, u32[]{:S(2)}, u32[]{:S(2)}) collective-permute-start(f32[3,1,1,1024]{3,2,1,0:T(1,128)S(1)} %get-tuple-element.24), channel_id=1, source_target_pairs={{0,1},{1,2},{2,3},{3,4},{4,5},{5,6},{6,7},{7,8},{8,9},{9,10},{10,1... | collective-permute-start | bytes 36872 | tf_op jit(solution)/shard_map/ppermute | solution.py:30
  14.7 11.1 %collective-permute-start.3 = (f32[3,1,1,1024]{3,2,1,0:T(1,128)S(1)}, f32[3,1,1,1024]{3,2,1,0:T(1,128)S(1)}, u32[]{:S(2)}, u32[]{:S(2)}) collective-permute-start(f32[3,1,1,1024]{3,2,1,0:T(1,128)S(1)} %get-tuple-element.25), channel_id=1, source_target_pairs={{1,0},{2,1},{3,2},{4,3},{5,4},{6,5},{7,6},{8,7},{9,8},{10,9},{11,1... | collective-permute-start | bytes 36872 | tf_op jit(solution)/shard_map/ppermute | solution.py:31
  23.8 1.3 copy-start.3
  27.2 1.5 copy-start.4
  29.1 1.6 copy-start.5
  35.1 1.9 %copy-start.1 = (bf16[16,15,1,64,64]{4,3,1,2,0:T(8,128)(2,1)}, bf16[16,15,1,64,64]{4,3,1,2,0:T(8,128)(2,1)S(1)}, u32[]{:S(2)}) copy-start(bf16[16,15,1,64,64]{4,3,1,2,0:T(8,128)(2,1)S(1)} %fusion.66) | copy-start | bytes 5898244
  134.1 24.1 %copy-start.2 = (bf16[3,1,1024,64]{2,3,1,0:T(8,128)(2,1)}, bf16[3,1,1024,64]{2,3,1,0:T(8,128)(2,1)S(1)}, u32[]{:S(2)}) copy-start(bf16[3,1,1024,64]{2,3,1,0:T(8,128)(2,1)S(1)} %get-tuple-element.8) | copy-start | bytes 1179652
  134.1 15.9 %collective-permute-start.6 = (bf16[3,1,1024,64]{2,3,1,0:T(8,128)(2,1)S(1)}, bf16[3,1,1024,64]{2,3,1,0:T(8,128)(2,1)S(1)}, u32[]{:S(2)}, u32[]{:S(2)}) collective-permute-start(bf16[3,1,1024,64]{2,3,1,0:T(8,128)(2,1)S(1)} %get-tuple-element.8), channel_id=1, source_target_pairs={{16,0},{32,16},{48,32},{64,48},{80,64},{96,80},{112,96},{128,112},... | collective-permute-start | bytes 1179656 | tf_op jit(solution)/shard_map/ppermute | solution.py:31
  141.4 16.3 %collective-permute-start.5 = (bf16[3,1,1024,64]{2,3,1,0:T(8,128)(2,1)S(1)}, bf16[3,1,1024,64]{2,3,1,0:T(8,128)(2,1)S(1)}, u32[]{:S(2)}, u32[]{:S(2)}) collective-permute-start(bf16[3,1,1024,64]{2,3,1,0:T(8,128)(2,1)S(1)} %get-tuple-element.8), channel_id=1, source_target_pairs={{0,16},{16,32},{32,48},{48,64},{64,80},{80,96},{96,112},{112,128},... | collective-permute-start | bytes 1179656 | tf_op jit(solution)/shard_map/ppermute | solution.py:30
  143.3 1.2 collective-permute-start.4
  143.4 3.4 %collective-permute-start.7 = (bf16[3,1,1024,1]{2,3,1,0:T(2,128)(2,1)S(1)}, bf16[3,1,1024,1]{2,3,1,0:T(2,128)(2,1)S(1)}, u32[]{:S(2)}, u32[]{:S(2)}) collective-permute-start(bf16[3,1,1024,1]{2,3,1,0:T(2,128)(2,1)S(1)} %get-tuple-element.18), channel_id=1, source_target_pairs={{1,0},{2,1},{3,2},{4,3},{5,4},{6,5},{7,6},{8,7},{9,8},{10,9},{11,1... | collective-permute-start | bytes 18440 | tf_op jit(solution)/shard_map/ppermute | solution.py:31
